TPU v7x, 32 devices: a whole 2x2x4 slice. The times are simulated.
32 devices in a mesh: dp: 32 (over z, y, x, core).
Axes of the slice: x: 2, y: 2, z: 4, core: 2. Of those that a mesh axis runs over, the one named last changes fastest.
Arguments:
- hidden_in: bfloat16 [128, 128, 768], P('dp'), may hold values from -6 to 6
- attention_keep: int32 [2, 128, 128, 768], P(None, 'dp'), may hold values 0 or 1
- feedforward_keep: int32 [2, 128, 128, 768], P(None, 'dp'), may hold values 0 or 1
- lengths: int32 [128], P('dp'), may hold values from 5 to 128, as said below
- cotangent: bfloat16 [2, 128, 128, 768], P(None, 'dp'), may hold values from -6 to 6
- query_weight: bfloat16 [768, 768], P('dp'), may hold values from -0.21875 to 0.21875
- key_weight: bfloat16 [768, 768], P('dp'), may hold values from -0.21875 to 0.21875
- value_weight: bfloat16 [768, 768], P('dp'), may hold values from -0.21875 to 0.21875
- output_weight: bfloat16 [768, 768], P('dp'), may hold values from -1.75 to 1.75
- inner_weight: bfloat16 [768, 3072], P('dp'), may hold values from -0.21875 to 0.21875
- outer_weight: bfloat16 [3072, 768], P('dp'), may hold values from -0.15625 to 0.15625
- pooler_weight: bfloat16 [768, 768], P('dp'), may hold values from -0.4375 to 0.4375
- query_bias: bfloat16 [768], P('dp'), may hold values from -3 to 3
- value_bias: bfloat16 [768], P('dp'), may hold values from -3 to 3
- output_bias: bfloat16 [768], P('dp'), may hold values from -3 to 3
- first_gain: bfloat16 [768], P('dp'), may hold values from 0.5 to 1.5
- first_shift: bfloat16 [768], P('dp'), may hold values from -3 to 3
- inner_bias: bfloat16 [3072], P('dp'), may hold values from -3 to 3
- outer_bias: bfloat16 [768], P('dp'), may hold values from -3 to 3
- second_gain: bfloat16 [768], P('dp'), may hold values from 0.5 to 1.5
- second_shift: bfloat16 [768], P('dp'), may hold values from -3 to 3
- pooler_bias: bfloat16 [768], P('dp'), may hold values from -3 to 3
Outputs:
- loss_value: float32 [], replicated
- hidden_out: bfloat16 [2, 128, 128, 768], P(None, 'dp')
- hidden_grad: float32 [128, 128, 768], P('dp')
- query_weight_grad: float32 [768, 768], P('dp')
- key_weight_grad: float32 [768, 768], P('dp')
- value_weight_grad: float32 [768, 768], P('dp')
- output_weight_grad: float32 [768, 768], P('dp')
- inner_weight_grad: float32 [768, 3072], P('dp')
- outer_weight_grad: float32 [3072, 768], P('dp')
- pooler_weight_grad: float32 [768, 768], P('dp')
- query_bias_grad: float32 [768], P('dp')
- value_bias_grad: float32 [768], P('dp')
- output_bias_grad: float32 [768], P('dp')
- first_gain_grad: float32 [768], P('dp')
- first_shift_grad: float32 [768], P('dp')
- inner_bias_grad: float32 [3072], P('dp')
- outer_bias_grad: float32 [768], P('dp')
- second_gain_grad: float32 [768], P('dp')
- second_shift_grad: float32 [768], P('dp')
- pooler_bias_grad: float32 [768], P('dp')
Inputs may be any that keep to these rules, and one draw needn't show every extreme that they name: `lengths`: a sentence's real tokens fill its first slots; some sentence has 128.
All inputs are finite; a program needn't handle non-finite values. No bound on the sum of `attention_keep` or of `feedforward_keep` on one device may be relied on, other than what follows from the above.
Results may differ from a plain program's by a relative error of at most 0.014.
Values may be sent and summed in bfloat16 or wider, within the bound.
No kernel may reach another device: no remote copies, remote signals or barrier semaphores. Data moves between devices by JAX's collectives and lax.ppermute only.
A program may use at most 192 MiB of HBM per device.

v0:
```python
import math

import jax
import jax.numpy as jnp
from jax import lax
from jax.sharding import PartitionSpec as P

HD = 64


keep_scale = 1.0 / 0.9
sharpening_divisor = 0.05
epsilon = 1e-12


def layer_norm(row_block, gain_row, shift_row):
    row_mean = jnp.mean(row_block, -1, keepdims=True)
    centred = row_block - row_mean
    variance = jnp.mean(centred * centred, -1, keepdims=True)
    return centred * lax.rsqrt(variance + epsilon) * gain_row + shift_row


def unit_vector(pre_act):
    tanh_out = jnp.tanh(pre_act)
    return tanh_out * lax.rsqrt(jnp.sum(tanh_out * tanh_out, -1, keepdims=True) + 1e-06)


def exact_gelu(inner_pre):
    return jax.nn.gelu(inner_pre, approximate=False)


def bilinear_multiply(left, right):
    return lax.dot_general(
        left, right, (((left.ndim - 1,), (0,)), ((), ())), preferred_element_type=jnp.float32
    )


def bilinear_multiply_flipped(left, right):
    return lax.dot_general(
        left, right, (((left.ndim - 1,), (1,)), ((), ())), preferred_element_type=jnp.float32
    )


def outer_sum(left, right):
    flat_left = left.reshape(-1, left.shape[-1])
    flat_right = right.reshape(-1, right.shape[-1])
    return lax.dot_general(
        flat_left, flat_right, (((0,), (0,)), ((), ())), preferred_element_type=jnp.float32
    )


def column_sum(rows_low):
    return jnp.sum(rows_low.astype(jnp.float32).reshape(-1, rows_low.shape[-1]), axis=0)


def attention_scores(queries, key_rows, key_valid):
    scores = jnp.einsum("gqhe,gkhe->ghqk", queries, key_rows, preferred_element_type=jnp.float32)
    scores = scores * (1.0 / math.sqrt(HD))
    return jnp.where(key_valid[:, None, None, :], scores, -1000000000.0)


def per_device(
    hidden_in,
    attention_keep,
    feedforward_keep,
    lengths,
    cotangent,
    query_weight,
    key_weight,
    value_weight,
    output_weight,
    inner_weight,
    outer_weight,
    pooler_weight,
    query_bias,
    value_bias,
    output_bias,
    first_gain,
    first_shift,
    inner_bias,
    outer_bias,
    second_gain,
    second_shift,
    pooler_bias,
):
    gathered = (
        lax.all_gather(query_weight, "dp", axis=0, tiled=True),
        lax.all_gather(key_weight, "dp", axis=0, tiled=True),
        lax.all_gather(value_weight, "dp", axis=0, tiled=True),
        lax.all_gather(output_weight, "dp", axis=0, tiled=True),
        lax.all_gather(inner_weight, "dp", axis=0, tiled=True),
        lax.all_gather(outer_weight, "dp", axis=0, tiled=True),
        lax.all_gather(pooler_weight, "dp", axis=0, tiled=True),
        lax.all_gather(query_bias, "dp", axis=0, tiled=True),
        lax.all_gather(value_bias, "dp", axis=0, tiled=True),
        lax.all_gather(output_bias, "dp", axis=0, tiled=True),
        lax.all_gather(first_gain, "dp", axis=0, tiled=True),
        lax.all_gather(first_shift, "dp", axis=0, tiled=True),
        lax.all_gather(inner_bias, "dp", axis=0, tiled=True),
        lax.all_gather(outer_bias, "dp", axis=0, tiled=True),
        lax.all_gather(second_gain, "dp", axis=0, tiled=True),
        lax.all_gather(second_shift, "dp", axis=0, tiled=True),
        lax.all_gather(pooler_bias, "dp", axis=0, tiled=True),
    )
    (
        query_full,
        key_full,
        value_full,
        output_full,
        inner_full,
        outer_full,
        pooler_full,
        query_bfull,
        value_bfull,
        output_bfull,
        gain_one,
        shift_one,
        inner_bfull,
        outer_bfull,
        gain_two,
        shift_two,
        pooler_bfull,
    ) = gathered
    sent_count, length, model_width = hidden_in.shape
    head_count = model_width // HD
    head_scale = 1.0 / math.sqrt(HD)
    key_valid = jnp.arange(length)[None, :] < lengths[:, None]
    queries = (
        (bilinear_multiply(hidden_in, query_full) + query_bfull)
        .astype(jnp.bfloat16)
        .reshape(sent_count, length, head_count, HD)
    )
    key_rows = (
        bilinear_multiply(hidden_in, key_full)
        .astype(jnp.bfloat16)
        .reshape(sent_count, length, head_count, HD)
    )
    value_rows = (
        (bilinear_multiply(hidden_in, value_full) + value_bfull)
        .astype(jnp.bfloat16)
        .reshape(sent_count, length, head_count, HD)
    )
    scores = attention_scores(queries, key_rows, key_valid)
    row_max = jnp.max(scores, -1, keepdims=True)
    log_total = row_max + jnp.log(jnp.sum(jnp.exp(scores - row_max), -1, keepdims=True))
    prob_low = jnp.exp(scores - log_total).astype(jnp.bfloat16)
    context = jnp.einsum(
        "ghqk,gkhe->gqhe", prob_low, value_rows, preferred_element_type=jnp.float32
    )
    context = context.reshape(sent_count, length, model_width).astype(jnp.bfloat16)
    attended = bilinear_multiply(context, output_full) + output_bfull
    keep_one = attention_keep.astype(jnp.float32)
    keep_two = feedforward_keep.astype(jnp.float32)
    first_in = hidden_in.astype(jnp.float32)[None] + attended[None] * keep_one * keep_scale
    first_out, first_pull = jax.vjp(
        layer_norm, first_in, gain_one.astype(jnp.float32), shift_one.astype(jnp.float32)
    )
    first_low = first_out.astype(jnp.bfloat16)
    inner_pre = bilinear_multiply(first_low, inner_full) + inner_bfull
    acted_rows, gelu_pull = jax.vjp(exact_gelu, inner_pre)
    acted_low = acted_rows.astype(jnp.bfloat16)
    outer_out = bilinear_multiply(acted_low, outer_full) + outer_bfull
    second_in = first_out + outer_out * keep_two * keep_scale
    second_out, second_pull = jax.vjp(
        layer_norm, second_in, gain_two.astype(jnp.float32), shift_two.astype(jnp.float32)
    )
    hidden_out = second_out.astype(jnp.bfloat16)
    pooled = second_out[:, :, 0, :].astype(jnp.bfloat16)
    pre_act = bilinear_multiply(pooled, pooler_full) + pooler_bfull
    length_scaled_embeddings, unit_pull = jax.vjp(unit_vector, pre_act)
    sphere_summed_embeddings = length_scaled_embeddings.astype(jnp.bfloat16)
    contrast_examples = lax.all_gather(sphere_summed_embeddings[1], "dp", axis=0, tiled=True)
    cosine_scores = (
        bilinear_multiply_flipped(sphere_summed_embeddings[0], contrast_examples)
        / sharpening_divisor
    )
    total_rows = contrast_examples.shape[0]
    targets = lax.axis_index("dp") * sent_count + jnp.arange(sent_count)
    is_target = jnp.arange(total_rows)[None, :] == targets[:, None]
    logit_max = jnp.max(cosine_scores, -1, keepdims=True)
    log_sums = logit_max + jnp.log(jnp.sum(jnp.exp(cosine_scores - logit_max), -1, keepdims=True))
    picked = jnp.sum(jnp.where(is_target, cosine_scores, 0.0), -1)
    loss_value = lax.psum(jnp.sum(log_sums[:, 0] - picked), "dp") / total_rows
    back_weights = (
        lax.all_gather(query_weight, "dp", axis=0, tiled=True),
        lax.all_gather(key_weight, "dp", axis=0, tiled=True),
        lax.all_gather(value_weight, "dp", axis=0, tiled=True),
        lax.all_gather(output_weight, "dp", axis=0, tiled=True),
        lax.all_gather(inner_weight, "dp", axis=0, tiled=True),
        lax.all_gather(outer_weight, "dp", axis=0, tiled=True),
        lax.all_gather(pooler_weight, "dp", axis=0, tiled=True),
    )
    query_back, key_back, value_back, output_back, inner_back, outer_back, pooler_back = (
        back_weights
    )
    row_share = 1.0 / total_rows
    softmax_rows = jnp.exp(cosine_scores - log_sums)
    cosine_score_derivative = (
        softmax_rows * row_share - jnp.where(is_target, row_share, 0.0)
    ).astype(jnp.bfloat16)
    matched_view_derivative = (
        bilinear_multiply(cosine_score_derivative, contrast_examples) / sharpening_divisor
    )
    firsts, row_logs = (
        lax.all_gather(
            sphere_summed_embeddings[0].astype(jnp.float32), "dp", axis=0, tiled=True
        ).astype(jnp.bfloat16),
        lax.all_gather(log_sums[:, 0], "dp", axis=0, tiled=True),
    )
    column_logits = (
        bilinear_multiply_flipped(firsts, sphere_summed_embeddings[1]) / sharpening_divisor
    )
    column_soft = jnp.exp(column_logits - row_logs[:, None])
    column_target = jnp.arange(total_rows)[:, None] == targets[None, :]
    column_grad = (column_soft * row_share - jnp.where(column_target, row_share, 0.0)).astype(
        jnp.bfloat16
    )
    far_grad = (
        lax.dot_general(
            column_grad, firsts, (((0,), (0,)), ((), ())), preferred_element_type=jnp.float32
        )
        / sharpening_divisor
    )
    (pre_grad,) = unit_pull(jnp.stack([matched_view_derivative, far_grad]))
    pre_low = pre_grad.astype(jnp.bfloat16)
    pooler_wgrad = outer_sum(pooled, pre_low)
    pooler_bgrad = column_sum(pre_low)
    pooled_back = bilinear_multiply_flipped(pre_low, pooler_back)
    out_grad = cotangent.astype(jnp.float32).at[:, :, 0, :].add(pooled_back)
    second_grad, gain_two_grad, shift_two_grad = second_pull(out_grad)
    outer_low = (second_grad * keep_two * keep_scale).astype(jnp.bfloat16)
    outer_wgrad = outer_sum(acted_low, outer_low)
    outer_bgrad = column_sum(outer_low)
    (inner_grad,) = gelu_pull(bilinear_multiply_flipped(outer_low, outer_back))
    inner_low = inner_grad.astype(jnp.bfloat16)
    inner_wgrad = outer_sum(first_low, inner_low)
    inner_bgrad = column_sum(inner_low)
    first_grad = second_grad + bilinear_multiply_flipped(inner_low, inner_back)
    in_grad, gain_one_grad, shift_one_grad = first_pull(first_grad)
    attended_low = jnp.sum(in_grad * keep_one * keep_scale, axis=0).astype(jnp.bfloat16)
    output_wgrad = outer_sum(context, attended_low)
    output_bgrad = column_sum(attended_low)
    context_grad = (
        bilinear_multiply_flipped(attended_low, output_back)
        .astype(jnp.bfloat16)
        .reshape(sent_count, length, head_count, HD)
    )
    again_scores = attention_scores(queries, key_rows, key_valid)
    prob_rows = jnp.exp(again_scores - log_total)
    prob_again = prob_rows.astype(jnp.bfloat16)
    value_grad = jnp.einsum(
        "ghqk,gqhe->gkhe", prob_again, context_grad, preferred_element_type=jnp.float32
    )
    prob_grad = jnp.einsum(
        "gqhe,gkhe->ghqk", context_grad, value_rows, preferred_element_type=jnp.float32
    )
    score_low = (
        prob_rows * (prob_grad - jnp.sum(prob_rows * prob_grad, -1, keepdims=True))
    ).astype(jnp.bfloat16)
    query_grad = (
        jnp.einsum("ghqk,gkhe->gqhe", score_low, key_rows, preferred_element_type=jnp.float32)
        * head_scale
    )
    key_grad = (
        jnp.einsum("ghqk,gqhe->gkhe", score_low, queries, preferred_element_type=jnp.float32)
        * head_scale
    )
    query_low = query_grad.astype(jnp.bfloat16).reshape(sent_count, length, model_width)
    key_low = key_grad.astype(jnp.bfloat16).reshape(sent_count, length, model_width)
    value_low = value_grad.astype(jnp.bfloat16).reshape(sent_count, length, model_width)
    query_wgrad = outer_sum(hidden_in, query_low)
    query_bgrad = column_sum(query_low)
    key_wgrad = outer_sum(hidden_in, key_low)
    value_wgrad = outer_sum(hidden_in, value_low)
    value_bgrad = column_sum(value_low)
    hidden_grad = (
        jnp.sum(in_grad, axis=0)
        + bilinear_multiply_flipped(query_low, query_back)
        + bilinear_multiply_flipped(key_low, key_back)
        + bilinear_multiply_flipped(value_low, value_back)
    )
    all_sums = (
        lax.psum_scatter(query_wgrad, "dp", scatter_dimension=0, tiled=True),
        lax.psum_scatter(key_wgrad, "dp", scatter_dimension=0, tiled=True),
        lax.psum_scatter(value_wgrad, "dp", scatter_dimension=0, tiled=True),
        lax.psum_scatter(output_wgrad, "dp", scatter_dimension=0, tiled=True),
        lax.psum_scatter(inner_wgrad, "dp", scatter_dimension=0, tiled=True),
        lax.psum_scatter(outer_wgrad, "dp", scatter_dimension=0, tiled=True),
        lax.psum_scatter(pooler_wgrad, "dp", scatter_dimension=0, tiled=True),
        lax.psum_scatter(query_bgrad, "dp", scatter_dimension=0, tiled=True),
        lax.psum_scatter(value_bgrad, "dp", scatter_dimension=0, tiled=True),
        lax.psum_scatter(output_bgrad, "dp", scatter_dimension=0, tiled=True),
        lax.psum_scatter(gain_one_grad, "dp", scatter_dimension=0, tiled=True),
        lax.psum_scatter(shift_one_grad, "dp", scatter_dimension=0, tiled=True),
        lax.psum_scatter(inner_bgrad, "dp", scatter_dimension=0, tiled=True),
        lax.psum_scatter(outer_bgrad, "dp", scatter_dimension=0, tiled=True),
        lax.psum_scatter(gain_two_grad, "dp", scatter_dimension=0, tiled=True),
        lax.psum_scatter(shift_two_grad, "dp", scatter_dimension=0, tiled=True),
        lax.psum_scatter(pooler_bgrad, "dp", scatter_dimension=0, tiled=True),
    )
    (
        query_sum,
        key_sum,
        value_sum,
        output_sum,
        inner_sum_w,
        outer_sum_w,
        pooler_sum,
        query_bsum,
        value_bsum,
        output_bsum,
        gain_one_sum,
        shift_one_sum,
        inner_bsum,
        outer_bsum,
        gain_two_sum,
        shift_two_sum,
        pooler_bsum,
    ) = all_sums
    return (
        loss_value,
        hidden_out,
        hidden_grad,
        query_sum,
        key_sum,
        value_sum,
        output_sum,
        inner_sum_w,
        outer_sum_w,
        pooler_sum,
        query_bsum,
        value_bsum,
        output_bsum,
        gain_one_sum,
        shift_one_sum,
        inner_bsum,
        outer_bsum,
        gain_two_sum,
        shift_two_sum,
        pooler_bsum,
    )


def solution(mesh):
    in_specs = (
        P("dp", None, None),
        P(None, "dp", None, None),
        P(None, "dp", None, None),
        P("dp"),
        P(None, "dp", None, None),
        P("dp", None),
        P("dp", None),
        P("dp", None),
        P("dp", None),
        P("dp", None),
        P("dp", None),
        P("dp", None),
        P("dp"),
        P("dp"),
        P("dp"),
        P("dp"),
        P("dp"),
        P("dp"),
        P("dp"),
        P("dp"),
        P("dp"),
        P("dp"),
    )
    out_specs = (
        P(),
        P(None, "dp", None, None),
        P("dp", None, None),
        P("dp", None),
        P("dp", None),
        P("dp", None),
        P("dp", None),
        P("dp", None),
        P("dp", None),
        P("dp", None),
        P("dp"),
        P("dp"),
        P("dp"),
        P("dp"),
        P("dp"),
        P("dp"),
        P("dp"),
        P("dp"),
        P("dp"),
        P("dp"),
    )
    return jax.shard_map(
        per_device, mesh=mesh, in_specs=in_specs, out_specs=out_specs, check_vma=False
    )
```

profile of v0, /device:TPU:0, one launch (start us, length us, event | category | flops | bytes accessed | tf_op | source)
XLA Modules:
  0.0 1422.1 jit_solution(9457089746367842013)
XLA Ops:
  20.4 42.4 %all-reduce.22 = (bf16[768]{0:T(1024)(128)(2,1)S(1)}, bf16[768]{0:T(1024)(128)(2,1)S(1)}, bf16[768]{0:T(1024)(128)(2,1)S(1)}, bf16[768]{0:T(1024)(128)(2,1)S(1)}...) all-reduce(bf16[768]{0:T(1024)(128)(2,1)S(1)} %dynamic-update-slice, ...), channel_id=1, replica_groups=mesh['dp'=32] {'dp'}, use_global_device_ids=true, to_apply=%add.9 | all-reduce | flops 9984 | bytes 39936
  63.5 2.5 convert_element_type.152
  66.6 1.9 convert_element_type.176
  68.5 2.0 add_convert_fusion.3
  71.7 51.7 %all-gather.12.cloned.1.call-done = bf16[768,768]{1,0:T(8,128)(2,1)} async-done(((bf16[24,768]{1,0:T(8,128)(2,1)}), bf16[768,768]{1,0:T(8,128)(2,1)}) %all-gather.12.cloned.1.call-update) | async-done | bytes 1179664 | tf_op jit(solution)/shard_map/all_gather | solution.py:87
  123.4 2.0 add_convert_fusion.2
  125.9 53.3 %all-gather.14.cloned.1.call-done = bf16[768,768]{1,0:T(8,128)(2,1)} async-done(((bf16[24,768]{1,0:T(8,128)(2,1)}), bf16[768,768]{1,0:T(8,128)(2,1)}) %all-gather.14.cloned.1.call-update) | async-done | bytes 1179664 | tf_op jit(solution)/shard_map/all_gather | solution.py:88
  179.2 2.0 convolution_convert_fusion.1
  184.3 1.9 convolution_convert_fusion.3
  186.2 48.6 %all-gather.16.cloned.1.call-done = bf16[768,768]{1,0:T(8,128)(2,1)} async-done(((bf16[24,768]{1,0:T(8,128)(2,1)}), bf16[768,768]{1,0:T(8,128)(2,1)}) %all-gather.16.cloned.1.call-update) | async-done | bytes 1179664 | tf_op jit(solution)/shard_map/all_gather | solution.py:90
  234.8 2.4 convolution_add_fusion
  238.0 2.6 multiply_reduce_fusion.7
  240.6 59.5 %all-gather.18.cloned.1.call-done = bf16[768,3072]{1,0:T(8,128)(2,1)} async-done(((bf16[24,3072]{1,0:T(8,128)(2,1)}), bf16[768,3072]{1,0:T(8,128)(2,1)}) %all-gather.18.cloned.1.call-update) | async-done | bytes 4718608 | tf_op jit(solution)/shard_map/all_gather | solution.py:91
  300.1 12.8 fusion.14
  312.9 4.5 copy-done.9
  317.4 30.1 %multiply_convert_fusion = (bf16[2,4,128,3072]{3,2,1,0:T(8,128)(2,1)}, f32[2,4,128,3072]{3,2,1,0:T(8,128)}) fusion(f32[2,4,128,3072]{3,2,1,0:T(8,128)S(1)} %get-tuple-element.163, f32[3072]{0:T(1024)S(1)} %convert_element_type.167, u8[2,128,3072]{2,1,0:T(8,128)(4,1)S(1)} %get-tuple-element.113, u8[2,128,3072]{2,1,0:T(8,128)(4,1)S(1)} %get-tuple-element.112), kind=kLoop, calls=%fused_computation.9 | loop fusion | flops 223346688 | bytes 33042432 | tf_op jit(solution)/shard_map/convert_element_type | solution.py:161
  347.4 17.4 %all-gather.20.cloned.1.call-done = bf16[3072,768]{1,0:T(8,128)(2,1)} async-done(((bf16[96,768]{1,0:T(8,128)(2,1)}), bf16[3072,768]{1,0:T(8,128)(2,1)}) %all-gather.20.cloned.1.call-update) | async-done | bytes 4718608 | tf_op jit(solution)/shard_map/all_gather | solution.py:92
  364.8 10.4 fusion.107
  377.5 42.5 %all-gather.22.cloned.1.call-done = bf16[768,768]{1,0:T(8,128)(2,1)} async-done(((bf16[24,768]{1,0:T(8,128)(2,1)}), bf16[768,768]{1,0:T(8,128)(2,1)}) %all-gather.22.cloned.1.call-update) | async-done | bytes 1179664 | tf_op jit(solution)/shard_map/all_gather | solution.py:93
  422.4 40.5 %all-gather = bf16[1,128,768]{2,0,1:T(2,128)(2,1)S(1)} all-gather(bf16[1,4,768]{2,0,1:T(2,128)(2,1)S(1)} %copy.109), channel_id=2, replica_groups=mesh['dp'=32] {'dp'}, dimensions={1}, use_global_device_ids=true | all-gather | bytes 202752 | tf_op jit(solution)/shard_map/all_gather | solution.py:172
  464.2 39.8 %all-gather.1 = bf16[32,4,768]{2,1,0:T(4,128)(2,1)} all-gather(bf16[1,4,768]{2,1,0:T(4,128)(2,1)S(1)} %get-tuple-element.159), channel_id=1, replica_groups=mesh['dp'=32] {'dp'}, dimensions={0}, use_global_device_ids=true | all-gather | bytes 202752 | tf_op jit(solution)/shard_map/all_gather | solution.py:205
  508.8 37.3 %all-reduce.10 = f32[128]{0:T(128)} all-reduce(f32[128]{0:T(128)} %copy-done.59), channel_id=1, replica_groups=mesh['dp'=32] {'dp'}, use_global_device_ids=true, to_apply=%add.10 | all-reduce | flops 128 | bytes 1024
  555.6 2.8 multiply_reduce_fusion
  560.4 1.8 convert_reduce_fusion.1
  562.2 18.3 %convert_reduce_fusion = (f32[3072]{0:T(1024)S(1)}, bf16[2,4,128,3072]{3,2,1,0:T(8,128)(2,1)}) fusion(f32[2,4,128,3072]{3,2,1,0:T(8,128)} %get-tuple-element.156, bf16[2,4,128,768]{3,2,1,0:T(8,128)(2,1)} %get-tuple-element.148, bf16[3072,768]{1,0:T(8,128)(2,1)} %all-gather.20.cloned.1.call-done, f32[2,4,128,3072]{3,2,1,0:T(8,128)} %copy-done.9, ...), kind=kOutput, calls=%fused_computation.7 | convolution fusion | flops 4885312512 | bytes 37773312 | tf_op jit(solution)/shard_map/dot_general | solution.py:39
  580.5 9.7 multiply_reduce_fusion.1
  596.4 2.3 copy.110
  598.7 2.7 multiply_reduce_fusion.2
  606.0 2.2 convolution_bitcast_fusion.6
  608.2 3.1 copy.139
  611.4 2.9 multiply_convert_fusion.3
  615.8 2.2 convolution_bitcast_fusion.5
  617.9 3.1 copy.141
  621.1 2.6 convert_reduce_fusion.3
  625.4 2.2 copy.143
  627.7 3.4 convolution_bitcast_fusion.3
  631.1 2.0 convolution_bitcast_fusion.2
  633.8 10.6 convolution_bitcast_fusion.1
  645.8 10.3 convolution_bitcast_fusion
  657.5 44.1 %all-reduce.21 = (f32[]{:T(128)}, f32[768]{0:T(1024)S(1)}, f32[768]{0:T(1024)S(1)}, f32[768]{0:T(1024)S(1)}, f32[768]{0:T(1024)S(1)}, /*index=5*/f32[768]{0:T(10...) all-reduce(f32[]{:T(128)} %subtract_reduce_fusion, ...), channel_id=1, replica_groups=mesh['dp'=32] {'dp'}, use_global_device_ids=true, to_apply=%region_11.12 | all-reduce | flops 9985 | bytes 79880 | tf_op jit(solution)/shard_map/psum | solution.py:183
  708.1 2.3 fusion.30
  711.3 2.0 add_add_fusion.3
  713.2 104.3 %reduce-scatter.24.cloned.1.call-done = f32[24,768]{1,0:T(8,128)} async-done(((f32[768,768]{1,0:T(8,128)}), f32[24,768]{1,0:T(8,128)}) %reduce-scatter.24.cloned.1.call-update) | async-done | bytes 73744
  817.5 104.3 %reduce-scatter.26.cloned.1.call-done = f32[24,768]{1,0:T(8,128)} async-done(((f32[768,768]{1,0:T(8,128)}), f32[24,768]{1,0:T(8,128)}) %reduce-scatter.26.cloned.1.call-update) | async-done | bytes 73744
  921.9 104.6 %reduce-scatter.14.cloned.1.call-done = f32[24,768]{1,0:T(8,128)} async-done(((f32[768,768]{1,0:T(8,128)}), f32[24,768]{1,0:T(8,128)}) %reduce-scatter.14.cloned.1.call-update) | async-done | bytes 73744 | tf_op jit(solution)/shard_map/reduce_scatter | solution.py:286
  1026.4 104.4 %reduce-scatter.20.cloned.1.call-done = f32[24,768]{1,0:T(8,128)} async-done(((f32[768,768]{1,0:T(8,128)}), f32[24,768]{1,0:T(8,128)}) %reduce-scatter.20.cloned.1.call-update) | async-done | bytes 73744 | tf_op jit(solution)/shard_map/reduce_scatter | solution.py:289
  1130.8 141.7 %reduce-scatter.16.cloned.1.call-done = f32[24,3072]{1,0:T(8,128)} async-done(((f32[768,3072]{1,0:T(8,128)}), f32[24,3072]{1,0:T(8,128)}) %reduce-scatter.16.cloned.1.call-update) | async-done | bytes 294928 | tf_op jit(solution)/shard_map/reduce_scatter | solution.py:287
  1272.5 141.5 %reduce-scatter.18.cloned.1.call-done = f32[96,768]{1,0:T(8,128)} async-done(((f32[3072,768]{1,0:T(8,128)}), f32[96,768]{1,0:T(8,128)}) %reduce-scatter.18.cloned.1.call-update) | async-done | bytes 294928 | tf_op jit(solution)/shard_map/reduce_scatter | solution.py:288
  (242 shorter events, 66.0 us)
Async XLA Ops:
  7.2 59.4 %copy-start.32 = (bf16[2,4,128,768]{3,2,1,0:T(8,128)(2,1)S(1)}, bf16[2,4,128,768]{3,2,1,0:T(8,128)(2,1)}, u32[]{:S(2)}) copy-start(bf16[2,4,128,768]{3,2,1,0:T(8,128)(2,1)} %param.28) | copy-start | bytes 4718596
  7.2 61.3 %all-gather.10.cloned.1.call-start = ((), (), s32[]{:S(2)}) async-start(), calls=%async_computation.7 | async-start | bytes 1216512 | tf_op jit(solution)/shard_map/all_gather | solution.py:89
  7.9 115.5 %all-gather.12.cloned.1.call-start = ((), (), s32[]{:S(2)}) async-start(), calls=%async_computation.8 | async-start | bytes 1216512 | tf_op jit(solution)/shard_map/all_gather | solution.py:87
  8.7 170.5 %all-gather.14.cloned.1.call-start = ((), (), s32[]{:S(2)}) async-start(), calls=%async_computation.9 | async-start | bytes 1216512 | tf_op jit(solution)/shard_map/all_gather | solution.py:88
  9.4 225.4 %all-gather.16.cloned.1.call-start = ((), (), s32[]{:S(2)}) async-start(), calls=%async_computation.10 | async-start | bytes 1216512 | tf_op jit(solution)/shard_map/all_gather | solution.py:90
  10.0 290.1 %all-gather.18.cloned.1.call-start = ((), (), s32[]{:S(2)}) async-start(), calls=%async_computation.11 | async-start | bytes 4866048 | tf_op jit(solution)/shard_map/all_gather | solution.py:91
  10.6 354.2 %all-gather.20.cloned.1.call-start = ((), (), s32[]{:S(2)}) async-start(), calls=%async_computation.12 | async-start | bytes 4866048 | tf_op jit(solution)/shard_map/all_gather | solution.py:92
  11.2 408.8 %all-gather.22.cloned.1.call-start = ((), (), s32[]{:S(2)}) async-start(), calls=%async_computation.13 | async-start | bytes 1216512 | tf_op jit(solution)/shard_map/all_gather | solution.py:93
  11.9 701.3 %reduce-scatter.22.cloned.1.call-start = ((), (), s32[]{:S(2)}) async-start(), calls=%async_computation.18 | async-start | bytes 2433024
  62.8 250.1 %copy-start.46 = (f32[3072]{0:T(1024)}, f32[3072]{0:T(1024)S(1)}, u32[]{:S(2)}) copy-start(f32[3072]{0:T(1024)S(1)} %convert_element_type.167) | copy-start | bytes 36868
  63.5 120.1 %copy-start.54 = (pred[4,128]{1,0:T(4,128)(4,1)}, pred[4,128]{1,0:T(4,128)(4,1)S(1)}, u32[]{:S(2)}) copy-start(pred[4,128]{1,0:T(4,128)(4,1)S(1)} %iota_compare_fusion.2) | copy-start | bytes 1540
  63.5 5.0 copy-start.12
  66.0 309.7 %copy-start.42 = (f32[768]{0:T(1024)}, f32[768]{0:T(1024)S(1)}, u32[]{:S(2)}) copy-start(f32[768]{0:T(1024)S(1)} %convert_element_type.171) | copy-start | bytes 9220
  125.9 56.8 %copy-start.16 = (bf16[4,128,768]{1,2,0:T(8,128)(2,1)}, bf16[4,128,768]{1,2,0:T(8,128)(2,1)S(1)}, u32[]{:S(2)}) copy-start(bf16[4,128,768]{1,2,0:T(8,128)(2,1)S(1)} %copy.105) | copy-start | bytes 2359300
  181.6 2.6 copy-start.28
  183.6 53.7 %copy-start.37 = (f32[4,12,128]{2,1,0:T(8,128)}, f32[4,12,128]{2,1,0:T(8,128)S(1)}, u32[]{:S(2)}) copy-start(f32[4,12,128]{2,1,0:T(8,128)S(1)} %log_add_fusion) | copy-start | bytes 73732
  184.3 53.0 %copy-start.3 = (s32[2,4,128,768]{3,2,1,0:T(8,128)S(1)}, s32[2,4,128,768]{3,2,1,0:T(8,128)}, u32[]{:S(2)}) copy-start(s32[2,4,128,768]{3,2,1,0:T(8,128)} %param.25) | copy-start | bytes 9437188
  240.6 72.3 %copy-start.48 = (f32[2,4,128]{2,1,0:T(4,128)}, f32[2,4,128]{2,1,0:T(4,128)S(1)}, u32[]{:S(2)}) copy-start(f32[2,4,128]{2,1,0:T(4,128)S(1)} %get-tuple-element.157) | copy-start | bytes 12292
  312.9 4.5 copy-start.9
  377.5 44.8 %copy-start.39 = (bf16[2,4,1,768]{3,2,1,0:T(2,128)(2,1)}, bf16[2,4,1,768]{3,2,1,0:T(2,128)(2,1)S(1)}, u32[]{:S(2)}) copy-start(bf16[2,4,1,768]{3,2,1,0:T(2,128)(2,1)S(1)} %slice.43) | copy-start | bytes 36868
  422.3 40.5 %copy-start.41 = (bf16[2,4,768]{2,1,0:T(4,128)(2,1)}, bf16[2,4,768]{2,1,0:T(4,128)(2,1)S(1)}, u32[]{:S(2)}) copy-start(bf16[2,4,768]{2,1,0:T(4,128)(2,1)S(1)} %multiply_convert_fusion.5) | copy-start | bytes 36868
  555.6 2.8 copy-start.51
  555.6 2.9 copy-start.2
  555.6 2.9 copy-start.43
  555.6 2.9 copy-start.45
  562.2 18.3 %copy-start.5 = (f32[2,4,128,768]{3,2,1,0:T(8,128)S(1)}, f32[2,4,128,768]{3,2,1,0:T(8,128)}, u32[]{:S(2)}) copy-start(f32[2,4,128,768]{3,2,1,0:T(8,128)} %get-tuple-element.158) | copy-start | bytes 9437188
  562.2 18.3 %copy-start.11 = (f32[2,4,128,768]{3,2,1,0:T(8,128)S(1)}, f32[2,4,128,768]{3,2,1,0:T(8,128)}, u32[]{:S(2)}) copy-start(f32[2,4,128,768]{3,2,1,0:T(8,128)} %copy-done.10) | copy-start | bytes 9437188
  580.5 9.7 copy-start.49
  592.1 2.6 copy-start.35
  593.9 4.8 copy-start.1
  593.9 4.8 copy-start.38
  593.9 4.8 copy-start.55
  611.3 206.2 %reduce-scatter.24.cloned.1.call-start = ((), (), s32[]{:S(2)}) async-start(), calls=%async_computation.19 | async-start | bytes 2433024
  611.4 4.4 copy-start.14
  621.1 300.8 %reduce-scatter.26.cloned.1.call-start = ((), (), s32[]{:S(2)}) async-start(), calls=%async_computation.20 | async-start | bytes 2433024
  621.1 3.5 copy-start.15
  627.6 3.5 copy-start.40
  627.6 398.8 %reduce-scatter.14.cloned.1.call-start = ((), (), s32[]{:S(2)}) async-start(), calls=%async_computation.14 | async-start | bytes 2433024 | tf_op jit(solution)/shard_map/reduce_scatter | solution.py:286
  631.1 2.8 copy-start.6
  631.1 499.7 %reduce-scatter.20.cloned.1.call-start = ((), (), s32[]{:S(2)}) async-start(), calls=%async_computation.17 | async-start | bytes 2433024 | tf_op jit(solution)/shard_map/reduce_scatter | solution.py:289
  633.1 639.3 %reduce-scatter.16.cloned.1.call-start = ((), (), s32[]{:S(2)}) async-start(), calls=%async_computation.15 | async-start | bytes 9732096 | tf_op jit(solution)/shard_map/reduce_scatter | solution.py:287
  644.4 769.5 %reduce-scatter.18.cloned.1.call-start = ((), (), s32[]{:S(2)}) async-start(), calls=%async_computation.16 | async-start | bytes 9732096 | tf_op jit(solution)/shard_map/reduce_scatter | solution.py:288
  656.1 52.0 %copy-start.27 = (bf16[4,12,64,128]{3,2,1,0:T(8,128)(2,1)S(1)}, bf16[4,12,64,128]{3,2,1,0:T(8,128)(2,1)}, u32[]{:S(2)}) copy-start(bf16[4,12,64,128]{3,2,1,0:T(8,128)(2,1)} %copy-done.26) | copy-start | bytes 2359300
  656.1 54.2 %copy-start.25 = (bf16[4,12,64,128]{3,2,1,0:T(8,128)(2,1)S(1)}, bf16[4,12,64,128]{3,2,1,0:T(8,128)(2,1)}, u32[]{:S(2)}) copy-start(bf16[4,12,64,128]{3,2,1,0:T(8,128)(2,1)} %copy-done.24) | copy-start | bytes 2359300
  701.6 8.8 copy-start.58
  708.1 3.1 copy-start.22
  708.1 3.1 copy-start.30
  708.1 3.1 copy-start.34
  (26 other events, 36.5 us)
Sparse Core Ops, SparseCore 0:
  10.9 56.7 all-gather.9
  70.6 52.7 all-gather.11
  126.4 52.8 all-gather.13
  182.0 52.8 all-gather.15
  237.6 62.4 all-gather.17
  302.8 61.9 all-gather.19
  367.7 52.2 all-gather.21
  611.4 101.6 reduce-scatter.21
  719.0 98.5 reduce-scatter.23
  823.2 98.5 reduce-scatter.25
  927.7 98.6 reduce-scatter.13
  1032.1 98.6 reduce-scatter.19
  1137.3 135.1 reduce-scatter.15
  1278.8 135.1 reduce-scatter.17
where the time goes:
time: 1430 us; the launch traced here: 1420 us
  waiting for transfers between devices  978 us (68%)
  blocking collectives  204 us (14%)
  matrix products  117 us (8%)
  other arithmetic  57.3 us (4%)
  local copies, waits for them, and re-layouts  47.8 us (3%)
  between operations  17 us (1%)
    unnamed x17, waiting for transfers between devices  213 us
    reduce_scatter x1, waiting for transfers between devices, per_device(): lax.psum_scatter(inner_wgrad, 'dp', scatter_dimension=0, tiled=True)  142 us
    reduce_scatter x1, waiting for transfers between devices, per_device(): lax.psum_scatter(outer_wgrad, 'dp', scatter_dimension=0, tiled=True)  142 us
    reduce_scatter x1, waiting for transfers between devices, per_device(): lax.psum_scatter(output_wgrad, 'dp', scatter_dimension=0, tiled=True)  105 us
    reduce_scatter x1, waiting for transfers between devices, per_device(): lax.psum_scatter(pooler_wgrad, 'dp', scatter_dimension=0, tiled=True)  104 us
    unnamed x2, blocking collectives  79.7 us
    all_gather x1, waiting for transfers between devices, per_device(): lax.all_gather(inner_weight, 'dp', axis=0, tiled=True)  59.5 us
    all_gather x1, waiting for transfers between devices, per_device(): lax.all_gather(key_weight, 'dp', axis=0, tiled=True)  53.3 us
  transfers between devices with their start and end apart: 14, of which 12 were waited for; matrix products, arithmetic and copies ran while one was open for 10% of the time, Pallas kernels for 0%

commit v1 on v0

--- a/solution.py
+++ b/solution.py
@@ -57,6 +57,31 @@
     scores = jnp.einsum("gqhe,gkhe->ghqk", queries, key_rows, preferred_element_type=jnp.float32)
     scores = scores * (1.0 / math.sqrt(HD))
     return jnp.where(key_valid[:, None, None, :], scores, -1000000000.0)
+
+
+def pack_shards(matrices, inner_weight, vectors, inner_bias):
+    width = matrices[0].shape[1]
+    row = jnp.concatenate(tuple(vectors) + (inner_bias,))
+    row = jnp.pad(row[None, :], ((0, 7), (0, width - row.shape[0])))
+    columns = [
+        inner_weight[:, place : place + width] for place in range(0, inner_weight.shape[1], width)
+    ]
+    return jnp.concatenate(list(matrices) + columns + [row], axis=0)
+
+
+def gather_doubling(block):
+    count = lax.axis_size("dp")
+    place = lax.axis_index("dp")
+    bits = count.bit_length() - 1
+    have = block[None]
+    for bit in reversed(range(bits)):
+        swap = [(source, source ^ (1 << bit)) for source in range(count)]
+        other = lax.ppermute(have, "dp", swap)
+        upper = ((place >> bit) & 1) == 1
+        low_half = jnp.where(upper, other, have)
+        high_half = jnp.where(upper, have, other)
+        have = jnp.stack((low_half, high_half), axis=1).reshape((-1,) + block.shape)
+    return have
 
 
 def per_device(
@@ -83,44 +108,63 @@
     second_shift,
     pooler_bias,
 ):
-    gathered = (
-        lax.all_gather(query_weight, "dp", axis=0, tiled=True),
-        lax.all_gather(key_weight, "dp", axis=0, tiled=True),
-        lax.all_gather(value_weight, "dp", axis=0, tiled=True),
-        lax.all_gather(output_weight, "dp", axis=0, tiled=True),
-        lax.all_gather(inner_weight, "dp", axis=0, tiled=True),
-        lax.all_gather(outer_weight, "dp", axis=0, tiled=True),
-        lax.all_gather(pooler_weight, "dp", axis=0, tiled=True),
-        lax.all_gather(query_bias, "dp", axis=0, tiled=True),
-        lax.all_gather(value_bias, "dp", axis=0, tiled=True),
-        lax.all_gather(output_bias, "dp", axis=0, tiled=True),
-        lax.all_gather(first_gain, "dp", axis=0, tiled=True),
-        lax.all_gather(first_shift, "dp", axis=0, tiled=True),
-        lax.all_gather(inner_bias, "dp", axis=0, tiled=True),
-        lax.all_gather(outer_bias, "dp", axis=0, tiled=True),
-        lax.all_gather(second_gain, "dp", axis=0, tiled=True),
-        lax.all_gather(second_shift, "dp", axis=0, tiled=True),
-        lax.all_gather(pooler_bias, "dp", axis=0, tiled=True),
+    device_count = lax.axis_size("dp")
+    packed = pack_shards(
+        (query_weight, key_weight, value_weight, output_weight, outer_weight, pooler_weight),
+        inner_weight,
+        (
+            query_bias,
+            value_bias,
+            output_bias,
+            first_gain,
+            first_shift,
+            outer_bias,
+            second_gain,
+            second_shift,
+            pooler_bias,
+        ),
+        inner_bias,
+    )
+    everyone = lax.all_gather(packed, "dp", axis=0, tiled=False)
+    shard_rows = query_weight.shape[0]
+    outer_rows = outer_weight.shape[0]
+    full_width = hidden_in.shape[-1]
+    starts = [0]
+    for rows in (shard_rows,) * 4 + (outer_rows, shard_rows):
+        starts.append(starts[-1] + rows)
+
+    def whole(place, rows):
+        return everyone[:, place : place + rows, :].reshape(device_count * rows, full_width)
+
+    query_full = whole(starts[0], shard_rows)
+    key_full = whole(starts[1], shard_rows)
+    value_full = whole(starts[2], shard_rows)
+    output_full = whole(starts[3], shard_rows)
+    outer_full = whole(starts[4], outer_rows)
+    pooler_full = whole(starts[5], shard_rows)
+    inner_parts = inner_weight.shape[1] // full_width
+    inner_full = jnp.concatenate(
+        [whole(starts[6] + part * shard_rows, shard_rows) for part in range(inner_parts)], axis=1
+    )
+    vector_row = everyone[:, starts[6] + inner_parts * shard_rows, :]
+    vectors = (
+        vector_row[:, : 9 * shard_rows]
+        .reshape(device_count, 9, shard_rows)
+        .transpose(1, 0, 2)
+        .reshape(9, full_width)
     )
     (
-        query_full,
-        key_full,
-        value_full,
-        output_full,
-        inner_full,
-        outer_full,
-        pooler_full,
         query_bfull,
         value_bfull,
         output_bfull,
         gain_one,
         shift_one,
-        inner_bfull,
         outer_bfull,
         gain_two,
         shift_two,
         pooler_bfull,
-    ) = gathered
+    ) = [vectors[place] for place in range(9)]
+    inner_bfull = vector_row[:, 9 * shard_rows : 9 * shard_rows + inner_bias.shape[0]].reshape(-1)
     sent_count, length, model_width = hidden_in.shape
     head_count = model_width // HD
     head_scale = 1.0 / math.sqrt(HD)
@@ -169,57 +213,41 @@
     pre_act = bilinear_multiply(pooled, pooler_full) + pooler_bfull
     length_scaled_embeddings, unit_pull = jax.vjp(unit_vector, pre_act)
     sphere_summed_embeddings = length_scaled_embeddings.astype(jnp.bfloat16)
-    contrast_examples = lax.all_gather(sphere_summed_embeddings[1], "dp", axis=0, tiled=True)
-    cosine_scores = (
-        bilinear_multiply_flipped(sphere_summed_embeddings[0], contrast_examples)
-        / sharpening_divisor
-    )
+    both_views = gather_doubling(sphere_summed_embeddings)
+    firsts = both_views[:, 0].reshape(-1, model_width)
+    contrast_examples = both_views[:, 1].reshape(-1, model_width)
+    cosine_scores = bilinear_multiply_flipped(firsts, contrast_examples) / sharpening_divisor
     total_rows = contrast_examples.shape[0]
-    targets = lax.axis_index("dp") * sent_count + jnp.arange(sent_count)
-    is_target = jnp.arange(total_rows)[None, :] == targets[:, None]
+    is_target = jnp.arange(total_rows)[None, :] == jnp.arange(total_rows)[:, None]
     logit_max = jnp.max(cosine_scores, -1, keepdims=True)
     log_sums = logit_max + jnp.log(jnp.sum(jnp.exp(cosine_scores - logit_max), -1, keepdims=True))
     picked = jnp.sum(jnp.where(is_target, cosine_scores, 0.0), -1)
-    loss_value = lax.psum(jnp.sum(log_sums[:, 0] - picked), "dp") / total_rows
-    back_weights = (
-        lax.all_gather(query_weight, "dp", axis=0, tiled=True),
-        lax.all_gather(key_weight, "dp", axis=0, tiled=True),
-        lax.all_gather(value_weight, "dp", axis=0, tiled=True),
-        lax.all_gather(output_weight, "dp", axis=0, tiled=True),
-        lax.all_gather(inner_weight, "dp", axis=0, tiled=True),
-        lax.all_gather(outer_weight, "dp", axis=0, tiled=True),
-        lax.all_gather(pooler_weight, "dp", axis=0, tiled=True),
-    )
-    query_back, key_back, value_back, output_back, inner_back, outer_back, pooler_back = (
-        back_weights
-    )
+    loss_value = jnp.sum(log_sums[:, 0] - picked) / total_rows
     row_share = 1.0 / total_rows
     softmax_rows = jnp.exp(cosine_scores - log_sums)
     cosine_score_derivative = (
         softmax_rows * row_share - jnp.where(is_target, row_share, 0.0)
     ).astype(jnp.bfloat16)
+    own_start = lax.axis_index("dp") * sent_count
+    own_rows = lax.dynamic_slice_in_dim(cosine_score_derivative, own_start, sent_count, 0)
+    own_columns = lax.dynamic_slice_in_dim(cosine_score_derivative, own_start, sent_count, 1)
     matched_view_derivative = (
-        bilinear_multiply(cosine_score_derivative, contrast_examples) / sharpening_divisor
-    )
-    firsts, row_logs = (
-        lax.all_gather(
-            sphere_summed_embeddings[0].astype(jnp.float32), "dp", axis=0, tiled=True
-        ).astype(jnp.bfloat16),
-        lax.all_gather(log_sums[:, 0], "dp", axis=0, tiled=True),
-    )
-    column_logits = (
-        bilinear_multiply_flipped(firsts, sphere_summed_embeddings[1]) / sharpening_divisor
-    )
-    column_soft = jnp.exp(column_logits - row_logs[:, None])
-    column_target = jnp.arange(total_rows)[:, None] == targets[None, :]
-    column_grad = (column_soft * row_share - jnp.where(column_target, row_share, 0.0)).astype(
-        jnp.bfloat16
+        bilinear_multiply(own_rows, contrast_examples) / sharpening_divisor
     )
     far_grad = (
         lax.dot_general(
-            column_grad, firsts, (((0,), (0,)), ((), ())), preferred_element_type=jnp.float32
+            own_columns, firsts, (((0,), (0,)), ((), ())), preferred_element_type=jnp.float32
         )
         / sharpening_divisor
+    )
+    query_back, key_back, value_back, output_back, inner_back, outer_back, pooler_back = (
+        query_full,
+        key_full,
+        value_full,
+        output_full,
+        inner_full,
+        outer_full,
+        pooler_full,
     )
     (pre_grad,) = unit_pull(jnp.stack([matched_view_derivative, far_grad]))
     pre_low = pre_grad.astype(jnp.bfloat16)
@@ -279,44 +307,80 @@
         + bilinear_multiply_flipped(key_low, key_back)
         + bilinear_multiply_flipped(value_low, value_back)
     )
-    all_sums = (
-        lax.psum_scatter(query_wgrad, "dp", scatter_dimension=0, tiled=True),
-        lax.psum_scatter(key_wgrad, "dp", scatter_dimension=0, tiled=True),
-        lax.psum_scatter(value_wgrad, "dp", scatter_dimension=0, tiled=True),
-        lax.psum_scatter(output_wgrad, "dp", scatter_dimension=0, tiled=True),
-        lax.psum_scatter(inner_wgrad, "dp", scatter_dimension=0, tiled=True),
-        lax.psum_scatter(outer_wgrad, "dp", scatter_dimension=0, tiled=True),
-        lax.psum_scatter(pooler_wgrad, "dp", scatter_dimension=0, tiled=True),
-        lax.psum_scatter(query_bgrad, "dp", scatter_dimension=0, tiled=True),
-        lax.psum_scatter(value_bgrad, "dp", scatter_dimension=0, tiled=True),
-        lax.psum_scatter(output_bgrad, "dp", scatter_dimension=0, tiled=True),
-        lax.psum_scatter(gain_one_grad, "dp", scatter_dimension=0, tiled=True),
-        lax.psum_scatter(shift_one_grad, "dp", scatter_dimension=0, tiled=True),
-        lax.psum_scatter(inner_bgrad, "dp", scatter_dimension=0, tiled=True),
-        lax.psum_scatter(outer_bgrad, "dp", scatter_dimension=0, tiled=True),
-        lax.psum_scatter(gain_two_grad, "dp", scatter_dimension=0, tiled=True),
-        lax.psum_scatter(shift_two_grad, "dp", scatter_dimension=0, tiled=True),
-        lax.psum_scatter(pooler_bgrad, "dp", scatter_dimension=0, tiled=True),
-    )
+    low = jnp.bfloat16
+
+    def split_rows(grad):
+        return grad.astype(low).reshape(device_count, -1, full_width)
+
+    vector_grads = jnp.stack(
+        (
+            query_bgrad,
+            value_bgrad,
+            output_bgrad,
+            gain_one_grad,
+            shift_one_grad,
+            outer_bgrad,
+            gain_two_grad,
+            shift_two_grad,
+            pooler_bgrad,
+        )
+    )
+    vector_part = (
+        vector_grads.reshape(9, device_count, shard_rows)
+        .transpose(1, 0, 2)
+        .reshape(device_count, 9 * shard_rows)
+    )
+    vector_part = jnp.concatenate((vector_part, inner_bgrad.reshape(device_count, -1)), axis=1)
+    vector_part = jnp.pad(
+        vector_part.astype(low)[:, None, :],
+        ((0, 0), (0, 7), (0, full_width - vector_part.shape[1])),
+    )
+    grads = jnp.concatenate(
+        [
+            split_rows(query_wgrad),
+            split_rows(key_wgrad),
+            split_rows(value_wgrad),
+            split_rows(output_wgrad),
+            split_rows(outer_wgrad),
+            split_rows(pooler_wgrad),
+        ]
+        + [
+            split_rows(inner_wgrad[:, part * full_width : (part + 1) * full_width])
+            for part in range(inner_parts)
+        ]
+        + [vector_part],
+        axis=1,
+    )
+    packed_rows = grads.shape[1]
+    sums = lax.psum_scatter(
+        grads.reshape(device_count * packed_rows, full_width), "dp", scatter_dimension=0, tiled=True
+    ).astype(jnp.float32)
+    query_sum = sums[starts[0] : starts[1]]
+    key_sum = sums[starts[1] : starts[2]]
+    value_sum = sums[starts[2] : starts[3]]
+    output_sum = sums[starts[3] : starts[4]]
+    outer_sum_w = sums[starts[4] : starts[5]]
+    pooler_sum = sums[starts[5] : starts[6]]
+    inner_sum_w = jnp.concatenate(
+        [
+            sums[starts[6] + part * shard_rows : starts[6] + (part + 1) * shard_rows]
+            for part in range(inner_parts)
+        ],
+        axis=1,
+    )
+    vector_sum = sums[starts[6] + inner_parts * shard_rows]
     (
-        query_sum,
-        key_sum,
-        value_sum,
-        output_sum,
-        inner_sum_w,
-        outer_sum_w,
-        pooler_sum,
         query_bsum,
         value_bsum,
         output_bsum,
         gain_one_sum,
         shift_one_sum,
-        inner_bsum,
         outer_bsum,
         gain_two_sum,
         shift_two_sum,
         pooler_bsum,
-    ) = all_sums
+    ) = [vector_sum[place * shard_rows : (place + 1) * shard_rows] for place in range(9)]
+    inner_bsum = vector_sum[9 * shard_rows : 9 * shard_rows + inner_bias.shape[0]]
     return (
         loss_value,
         hidden_out,

time: 1430 us -> 577 us (0.40)
  waiting for transfers between devices: 978 us -> 285 us
  blocking collectives: 204 us -> 0 us
  local copies, waits for them, and re-layouts: 47.8 us -> 96.1 us
    reduce_scatter x4 -> x1, waiting for transfers between devices: 492 us -> 163 us  [per_device(): lax.psum_scatter(grads.reshape(device_count * packed_rows, full_width), '...]
    unnamed x17 -> x2, waiting for transfers between devices: 213 us -> 0.03 us
    all_gather x7 -> x1, waiting for transfers between devices: 273 us -> 110 us  [per_device(): everyone = lax.all_gather(packed, 'dp', axis=0, tiled=False)]
    all_gather x2 -> x0, blocking collectives: 80.3 us -> none  [the longest x1 40.5 us: per_device(): lax.all_gather(sphere_summed_embeddings[1], 'dp', axis=0, tiled=True)]
    unnamed x2 -> x0, blocking collectives: 79.7 us -> none
    psum x1 -> x0, blocking collectives: 44.1 us -> none  [per_device(): loss_value = lax.psum(jnp.sum(log_sums[:, 0] - picked), 'dp') / total_rows]
    slice x2 -> x11, local copies, waits for them, and re-layouts: 0.02 us -> 21.6 us  [the longest x2 12.4 us: whole(): everyone[:, place:place + rows, :].reshape(device_count * rows, full_width)]
    unnamed x154 -> x174, local copies, waits for them, and re-layouts: 38.2 us -> 41.3 us
  transfers between devices with their start and end apart: 14 -> 7, of which waited for: 12 -> 6; matrix products, arithmetic and copies ran while one was open for 10% -> 2% of each run, Pallas kernels for 0% -> 0%
where the time goes in v1:
time: 577 us; the launch traced here: 568 us
  waiting for transfers between devices  285 us (49%)
  matrix products  104 us (18%)
  local copies, waits for them, and re-layouts  96.1 us (17%)
  other arithmetic  60.2 us (10%)
  between operations  17.5 us (3%)
    reduce_scatter x1, waiting for transfers between devices, per_device(): lax.psum_scatter(grads.reshape(device_count * packed_rows, full_width), '...  163 us
    all_gather x1, waiting for transfers between devices, per_device(): everyone = lax.all_gather(packed, 'dp', axis=0, tiled=False)  110 us
    unnamed x174, local copies, waits for them, and re-layouts  41.3 us
    dot_general x8, matrix products, bilinear_multiply_flipped(): lax.dot_general(left, right, (((left.ndim - 1,), (1,)), ((), ())), prefer...  40.8 us
    convert_element_type x1, other arithmetic, per_device(): acted_low = acted_rows.astype(jnp.bfloat16)  32.1 us
    dot_general x8, matrix products, bilinear_multiply(): lax.dot_general(left, right, (((left.ndim - 1,), (0,)), ((), ())), prefer...  28.3 us
    dot_general x7, matrix products, outer_sum(): lax.dot_general(flat_left, flat_right, (((0,), (0,)), ((), ())), preferre...  22.8 us
    slice x2, local copies, waits for them, and re-layouts, whole(): everyone[:, place:place + rows, :].reshape(device_count * rows, full_width)  12.4 us
  transfers between devices with their start and end apart: 7, of which 6 were waited for; matrix products, arithmetic and copies ran while one was open for 2% of the time, Pallas kernels for 0%

profile of v1, /device:TPU:0, one launch (start us, length us, event | category | flops | bytes accessed | tf_op | source)
XLA Modules:
  0.0 567.8 jit_solution(6437536758878637458)
XLA Ops:
  7.2 6.8 %concatenate.34 = bf16[312]{0:T(512)(128)(2,1)S(1)} concatenate(bf16[24]{0:T(256)(128)(2,1)} %param.36, bf16[24]{0:T(256)(128)(2,1)} %param.37, bf16[24]{0:T(256)(128)(2,1)} %param.38, bf16[24]{0:T(256)(128)(2,1)} %param.39, bf16[24]{0:T(256)(128)(2,1)} %param.40, bf16[24]{0:T(256)(128)(2,1)} %param.42, bf16[24]{0:T(256)(128)(2,1)} %param.43, bf16[24]{0:T(256)(128)(2,1)} %param.44, ...), dimensions={0} | concatenate | bytes 1248 | tf_op jit(solution)/shard_map/concatenate | solution.py:64
  22.8 2.4 convert_element_type.275
  25.2 109.9 %all-gather.3.cloned.1.call-done = bf16[10240,768]{1,0:T(8,128)(2,1)} async-done(((bf16[320,768]{1,0:T(8,128)(2,1)}), bf16[10240,768]{1,0:T(8,128)(2,1)}) %all-gather.3.cloned.1.call-update) | async-done | bytes 15728656 | tf_op jit(solution)/shard_map/all_gather | solution.py:128
  136.3 4.8 slice.320
  141.1 7.6 %fusion.56 = (bf16[32,24,768]{2,1,0:T(8,128)(2,1)}, bf16[32,24,768]{2,1,0:T(8,128)(2,1)}, bf16[32,24,768]{2,1,0:T(8,128)(2,1)}, bf16[32,24,768]{2,1,0:T(8,128)(2...) fusion(bf16[32,320,768]{2,1,0:T(8,128)(2,1)} %bitcast.243), kind=kLoop, calls=%fused_computation.204 | loop fusion | bytes 21233664 | tf_op jit(solution)/shard_map/slice | solution.py:137
  162.2 14.2 %fusion.7 = (u8[2,128,3072]{2,1,0:T(8,128)(4,1)}, u8[2,128,3072]{2,1,0:T(8,128)(4,1)}, f32[2,4,128,3072]{3,2,1,0:T(8,128)}) fusion(f32[3072]{0:T(1024)S(1)} %reshape.530, bf16[768,768]{1,0:T(8,128)(2,1)S(1)} %bitcast.286, bf16[768,768]{1,0:T(8,128)(2,1)S(1)} %bitcast.288, bf16[768,768]{1,0:T(8,128)(2,1)S(1)} %bitcast.290, ...), kind=kOutput, calls=%fused_computation.44 | convolution fusion | flops 4896325632 | bytes 22042624 | tf_op jit(solution)/shard_map/dot_general | solution.py:33
  176.4 32.1 %multiply_convert_fusion = (bf16[2,4,128,3072]{3,2,1,0:T(8,128)(2,1)S(1)}, f32[2,4,128,3072]{3,2,1,0:T(8,128)}) fusion(f32[2,4,128,3072]{3,2,1,0:T(8,128)} %get-tuple-element.112, f32[3072]{0:T(1024)S(1)} %reshape.530, u8[2,128,3072]{2,1,0:T(8,128)(4,1)} %get-tuple-element.33, u8[2,128,3072]{2,1,0:T(8,128)(4,1)} %get-tuple-element.32), kind=kLoop, calls=%fused_computation.8 | loop fusion | flops 223346688 | bytes 33042432 | tf_op jit(solution)/shard_map/convert_element_type | solution.py:205
  208.6 10.2 %fusion.60 = (f32[2,4,128]{2,1,0:T(4,128)S(1)}, f32[2,4,128,768]{3,2,1,0:T(8,128)S(1)}) fusion(s32[2,4,128,768]{3,2,1,0:T(8,128)S(1)} %copy-done.26, f32[768]{0:T(1024)S(1)} %reshape.531, bf16[2,4,128,3072]{3,2,1,0:T(8,128)(2,1)S(1)} %get-tuple-element.54, bf16[3072,768,1,1]{1,0,3,2:T(8,128)(2,1)} %bitcast.252, f32[768]{0:T(1024)S(1)} %reshape.529, ...), kind=kOutput, calls=%fused_computation.208 | convolution fusion | flops 4838915072 | bytes 20464640 | tf_op jit(solution)/shard_map/dot_general | solution.py:33
  222.2 1.5 collective-permute-start
  223.7 3.1 collective-permute-done
  227.7 3.1 collective-permute-done.1
  230.9 1.5 collective-permute-start.2
  232.5 2.6 collective-permute-done.2
  235.3 1.5 collective-permute-start.3
  236.8 3.2 collective-permute-done.3
  240.4 3.5 convert_element_type.314
  250.0 1.7 fusion.63
  251.7 2.3 bitcast_convert_fusion.2
  255.0 1.7 scatter-add.4
  256.7 3.6 multiply_reduce_fusion
  265.5 7.2 %bitcast_convert_fusion.1 = bf16[3072,768]{1,0:T(8,128)(2,1)} fusion(bf16[2,4,128,3072]{3,2,1,0:T(8,128)(2,1)S(1)} %bitcast.247, bf16[2,4,128,768]{3,2,1,0:T(8,128)(2,1)S(1)} %get-tuple-element.47), kind=kOutput, calls=%fused_computation.22 | convolution fusion | flops 4834197504 | bytes 12582912 | tf_op jit(solution)/shard_map/dot_general | solution.py:47
  272.7 19.0 %fusion.62 = (bf16[3072]{0:T(1024)(128)(2,1)}, bf16[2,4,128,3072]{3,2,1,0:T(8,128)(2,1)}) fusion(f32[2,4,128,3072]{3,2,1,0:T(8,128)} %get-tuple-element.55, bf16[2,4,128,768]{3,2,1,0:T(8,128)(2,1)} %copy-done.31, bf16[3072,768,1,1]{1,0,3,2:T(8,128)(2,1)} %bitcast.253, f32[2,4,128,3072]{3,2,1,0:T(8,128)} %get-tuple-element.112, f32[3072]{0:T(1024)S(1)} %copy-done.53), kind=kOutput, calls=%fused_computation.210 | convolution fusion | flops 4882166784 | bytes 37767168 | tf_op jit(solution)/shard_map/dot_general | solution.py:39
  291.7 13.1 %multiply_reduce_fusion.1 = (bf16[768]{0:T(1024)(128)(2,1)}, f32[2,4,128]{2,1,0:T(4,128)S(1)}, bf16[768]{0:T(1024)(128)(2,1)}, f32[2,4,128,768]{3,2,1,0:T(8,128)S(1)}) fusion(f32[2,4,128,768]{3,2,1,0:T(8,128)S(1)} %copy-done.7, f32[2,4,128]{2,1,0:T(4,128)S(1)} %copy-done.60, f32[768]{0:T(1024)S(1)} %copy-done.57, ...), kind=kOutput, calls=%fused_computation.27 | convolution fusion | flops 4857787392 | bytes 20465664 | tf_op jit(solution)/shard_map/dot_general | solution.py:39
  304.8 7.6 %bitcast_convert_fusion = bf16[768,3072]{1,0:T(8,128)(2,1)} fusion(bf16[2,4,128,3072]{3,2,1,0:T(8,128)(2,1)S(1)} %copy-done.67, f32[2,4,128,768]{3,2,1,0:T(8,128)S(1)} %copy-done.7, f32[768]{0:T(1024)S(1)} %copy-done.65, f32[768]{0:T(1024)S(1)} %copy-done.57, f32[2,4,128]{2,1,0:T(4,128)S(1)} %copy-done.60), kind=kOutput, calls=%fused_computation.21 | convolution fusion | flops 4837343232 | bytes 14166016 | tf_op jit(solution)/shard_map/dot_general | solution.py:47
  314.4 1.7 add_reduce_fusion
  316.1 1.7 convolution_convert_fusion.3
  318.6 1.8 bitcast_convert_fusion.3
  320.4 2.3 copy.181
  322.7 4.0 bitcast_reduce_fusion
  326.7 1.4 multiply_reduce_fusion.2
  329.3 2.1 multiply_convert_fusion.3
  331.3 2.0 bitcast_reduce_fusion.1
  334.2 3.7 fusion.57
  337.9 1.4 concatenate.38
  339.3 1.4 stack.104
  340.7 1.4 stack.105
  342.1 1.4 stack.107
  344.7 1.4 stack.103
  346.1 2.7 copy.190
  348.7 1.4 stack.102
  360.4 1.6 copy.193
  363.8 1.8 copy.189
  365.5 2.3 convolution_convert_fusion
  375.0 2.5 constant_dynamic-update-slice_fusion.25
  385.7 2.2 fusion.65
  388.8 2.0 add_add_fusion.3
  390.8 163.1 %reduce-scatter.2.cloned.1.call-done = bf16[320,768]{1,0:T(8,128)(2,1)} async-done(((bf16[10240,768]{1,0:T(8,128)(2,1)}), bf16[320,768]{1,0:T(8,128)(2,1)}) %reduce-scatter.2.cloned.1.call-update) | async-done | bytes 491536 | tf_op jit(solution)/shard_map/reduce_scatter | solution.py:355
  556.3 1.6 fusion.58
  (282 shorter events, 77.6 us)
Async XLA Ops:
  7.2 18.0 %copy-start.66 = (s32[4]{0:T(128)S(1)}, s32[4]{0:T(128)}, u32[]{:S(2)}) copy-start(s32[4]{0:T(128)} %param.27) | copy-start | bytes 52
  7.2 127.9 %all-gather.3.cloned.1.call-start = ((), (), s32[]{:S(2)}) async-start(), calls=%async_computation.2 | async-start | bytes 16220160 | tf_op jit(solution)/shard_map/all_gather | solution.py:128
  22.7 531.2 %reduce-scatter.2.cloned.1.call-start = ((), (), s32[]{:S(2)}) async-start(), calls=%async_computation.1 | async-start | bytes 16220160 | tf_op jit(solution)/shard_map/reduce_scatter | solution.py:355
  25.2 129.8 %copy-start.62 = (pred[4,128]{1,0:T(4,128)(4,1)}, pred[4,128]{1,0:T(4,128)(4,1)S(1)}, u32[]{:S(2)}) copy-start(pred[4,128]{1,0:T(4,128)(4,1)S(1)} %iota_compare_fusion.1) | copy-start | bytes 1540
  141.1 9.4 %copy-start.40 = (bf16[4,128,768]{2,1,0:T(8,128)(2,1)S(1)}, bf16[4,128,768]{2,1,0:T(8,128)(2,1)}, u32[]{:S(2)}) copy-start(bf16[4,128,768]{2,1,0:T(8,128)(2,1)} %param.24) | copy-start | bytes 2359300
  148.8 27.7 %copy-start.52 = (f32[3072]{0:T(1024)}, f32[3072]{0:T(1024)S(1)}, u32[]{:S(2)}) copy-start(f32[3072]{0:T(1024)S(1)} %reshape.530) | copy-start | bytes 36868
  149.7 58.8 %copy-start.64 = (f32[768]{0:T(1024)}, f32[768]{0:T(1024)S(1)}, u32[]{:S(2)}) copy-start(f32[768]{0:T(1024)S(1)} %reshape.529) | copy-start | bytes 9220
  149.9 58.6 %copy-start.56 = (f32[768]{0:T(1024)}, f32[768]{0:T(1024)S(1)}, u32[]{:S(2)}) copy-start(f32[768]{0:T(1024)S(1)} %reshape.528) | copy-start | bytes 9220
  155.0 3.2 copy-start.5
  158.9 3.3 copy-start.39
  159.9 48.7 %copy-start.6 = (f32[2,4,128,768]{3,2,1,0:T(8,128)}, f32[2,4,128,768]{3,2,1,0:T(8,128)S(1)}, u32[]{:S(2)}) copy-start(f32[2,4,128,768]{3,2,1,0:T(8,128)S(1)} %get-tuple-element.57) | copy-start | bytes 9437188
  159.9 48.7 %copy-start.59 = (f32[2,4,128]{2,1,0:T(4,128)}, f32[2,4,128]{2,1,0:T(4,128)S(1)}, u32[]{:S(2)}) copy-start(f32[2,4,128]{2,1,0:T(4,128)S(1)} %fusion.36) | copy-start | bytes 12292
  176.4 32.1 %copy-start.26 = (s32[2,4,128,768]{3,2,1,0:T(8,128)S(1)}, s32[2,4,128,768]{3,2,1,0:T(8,128)}, u32[]{:S(2)}) copy-start(s32[2,4,128,768]{3,2,1,0:T(8,128)} %param.26) | copy-start | bytes 9437188
  208.5 10.3 %copy-start.10 = (bf16[2,4,128,3072]{3,2,1,0:T(8,128)(2,1)}, bf16[2,4,128,3072]{3,2,1,0:T(8,128)(2,1)S(1)}, u32[]{:S(2)}) copy-start(bf16[2,4,128,3072]{3,2,1,0:T(8,128)(2,1)S(1)} %get-tuple-element.54) | copy-start | bytes 18874372
  220.4 3.3 copy-start.51
  221.6 18.5 %copy-start.47 = (f32[2,4,768]{2,1,0:T(4,128)}, f32[2,4,768]{2,1,0:T(4,128)S(1)}, u32[]{:S(2)}) copy-start(f32[2,4,768]{2,1,0:T(4,128)S(1)} %get-tuple-element.116) | copy-start | bytes 73732
  222.1 4.8 copy-start.58
  222.2 4.6 collective-permute-start
  226.9 3.9 collective-permute-start.1
  230.9 4.2 collective-permute-start.2
  235.3 4.7 collective-permute-start.3
  240.3 3.5 collective-permute-start.4
  254.0 6.3 %copy-start.55 = (f32[2,4,128]{2,1,0:T(4,128)S(1)}, f32[2,4,128]{2,1,0:T(4,128)}, u32[]{:S(2)}) copy-start(f32[2,4,128]{2,1,0:T(4,128)} %copy-done.54) | copy-start | bytes 12292
  256.7 3.8 copy-start.1
  256.7 4.7 copy-start.2
  256.7 8.0 %slice-start = ((s8[6291456]{0:T(1024)(128)(4,1)}), s8[4194304]{0:T(1024)(128)(4,1)S(1)}, s32[]{:S(2)}) async-start(s8[6291456]{0:T(1024)(128)(4,1)} %bitcast.246), calls=%async_computation.3 | async-start | bytes 8388608
  261.4 4.1 slice-start.1
  264.7 8.0 %copy-start.31 = (bf16[2,4,128,768]{3,2,1,0:T(8,128)(2,1)}, bf16[2,4,128,768]{3,2,1,0:T(8,128)(2,1)S(1)}, u32[]{:S(2)}) copy-start(bf16[2,4,128,768]{3,2,1,0:T(8,128)(2,1)S(1)} %get-tuple-element.47) | copy-start | bytes 4718596
  265.5 7.2 %copy-start.53 = (f32[3072]{0:T(1024)S(1)}, f32[3072]{0:T(1024)}, u32[]{:S(2)}) copy-start(f32[3072]{0:T(1024)} %copy-done.52) | copy-start | bytes 36868
  272.7 19.0 %copy-start.7 = (f32[2,4,128,768]{3,2,1,0:T(8,128)S(1)}, f32[2,4,128,768]{3,2,1,0:T(8,128)}, u32[]{:S(2)}) copy-start(f32[2,4,128,768]{3,2,1,0:T(8,128)} %copy-done.6) | copy-start | bytes 9437188
  272.7 19.0 %copy-start.57 = (f32[768]{0:T(1024)S(1)}, f32[768]{0:T(1024)}, u32[]{:S(2)}) copy-start(f32[768]{0:T(1024)} %copy-done.56) | copy-start | bytes 9220
  272.7 19.0 %copy-start.60 = (f32[2,4,128]{2,1,0:T(4,128)S(1)}, f32[2,4,128]{2,1,0:T(4,128)}, u32[]{:S(2)}) copy-start(f32[2,4,128]{2,1,0:T(4,128)} %copy-done.59) | copy-start | bytes 12292
  291.7 13.1 %copy-start.65 = (f32[768]{0:T(1024)S(1)}, f32[768]{0:T(1024)}, u32[]{:S(2)}) copy-start(f32[768]{0:T(1024)} %copy-done.64) | copy-start | bytes 9220
  291.7 13.1 %copy-start.67 = (bf16[2,4,128,3072]{3,2,1,0:T(8,128)(2,1)S(1)}, bf16[2,4,128,3072]{3,2,1,0:T(8,128)(2,1)}, u32[]{:S(2)}) copy-start(bf16[2,4,128,3072]{3,2,1,0:T(8,128)(2,1)} %get-tuple-element.123) | copy-start | bytes 18874372
  317.8 4.9 copy-start.50
  317.8 4.9 copy-start.63
  322.7 4.0 copy-start.29
  322.7 4.0 copy-start.46
  362.9 4.9 copy-start.42
  365.5 3.1 copy-start.24
  368.7 6.3 %slice-start.2 = ((s8[4718592]{0:T(1024)(128)(4,1)}), s8[4194304]{0:T(1024)(128)(4,1)S(1)}, s32[]{:S(2)}) async-start(s8[4718592]{0:T(1024)(128)(4,1)} %bitcast.254), calls=%async_computation.5 | async-start | bytes 8388608
  370.4 3.5 copy-start.32
  370.4 4.6 slice-start.3
  384.6 3.4 copy-start.25
  384.6 3.4 copy-start.34
  385.7 3.1 copy-start.15
  385.7 3.1 copy-start.28
  553.9 4.7 copy-start.18
  (31 other events, 52.8 us)
Sparse Core Ops, SparseCore 0:
  22.8 112.2 all-gather.2
  384.7 169.1 reduce-scatter.1
